TPU v7x, 128 devices: a whole 4x4x4 slice. The times are simulated.
128 devices in a mesh: dp: 16 (over z, y), tensor: 8 (over x, core).
Axes of the slice: x: 4, y: 4, z: 4, core: 2. Of those that a mesh axis runs over, the one named last changes fastest.
Arguments:
- dense: bfloat16 [3072, 2048], P('dp'), may hold values from -8 to 8
- bottom_weight: bfloat16 [2048, 16384], P(None, 'tensor'), may hold values from -0.125 to 0.125
- bottom_bias: float32 [16384], P('tensor'), may hold values from -3 to 3
- cross_blocks: bfloat16 [80, 512, 512], P('tensor', 'dp'), may hold values from -0.25 to 0.25
- cross_bias: float32 [16384], P('tensor'), may hold values from -3 to 3
- cotangent: bfloat16 [3072, 16384], P('dp', 'tensor'), may hold values from -6 to 6
- in_blocks: int32 [8, 10], replicated, may hold values from 0 to 31, as said below
- out_blocks: int32 [8, 10], replicated, may hold values from 0 to 31, as said below
- live_slots: int32 [8], replicated, may hold values from 2 to 10, as said below
Outputs:
- cross_out: bfloat16 [3072, 16384], P('dp', 'tensor')
- grad_bottom: float32 [2048, 16384], P('dp', 'tensor')
- grad_bias_bottom: float32 [16384], P('tensor')
- grad_blocks: float32 [80, 512, 512], P('tensor', 'dp')
- grad_bias: float32 [16384], P('tensor')
Inputs may be any that keep to these rules, and one draw needn't show every extreme that they name: `in_blocks`: among the live slots of one tensor device, at most 2 have input blocks held by any one tensor device (blocks s * 16384 / (512 * 8) onward for device s), and this most is reached in every draw. `out_blocks`: among the live slots of one tensor device, at most 2 have output blocks held by any one tensor device, and this most is reached in every draw. `live_slots`: some tensor device has all 10 slots live.
All inputs are finite; a program needn't handle non-finite values.
Results may differ from a plain program's by a relative error of at most 0.014.
Values may be sent and summed in bfloat16 or wider, within the bound.
A program may use at most 128 MiB of HBM per device.

v0:
```python
import jax
import jax.numpy as jnp
from jax import lax
from jax.sharding import PartitionSpec as P

BLK = 512
SLOTS = 10


def slot_ranks(owner, alive):
    order = jnp.arange(owner.shape[1])
    earlier = order[None, :] < order[:, None]
    same = (owner[:, :, None] == owner[:, None, :]) & alive[:, None, :] & earlier[None, :, :]
    return jnp.sum(same.astype(jnp.int32), axis=2)


def post_table(owner_mine, rank_mine, alive_mine, groups, capacity):
    slot_count = owner_mine.shape[0]
    match = (
        (owner_mine[None, None, :] == jnp.arange(groups)[:, None, None])
        & (rank_mine[None, None, :] == jnp.arange(capacity)[None, :, None])
        & alive_mine[None, None, :]
    )
    chosen = jnp.sum(match.astype(jnp.int32) * jnp.arange(slot_count)[None, None, :], axis=2)
    filled = jnp.any(match, axis=2)
    return (chosen, filled)


def pack_parts(parts, chosen, filled):
    picked = jnp.take(parts, chosen.reshape(-1), axis=1) * filled.reshape(-1)[None, :, None].astype(
        parts.dtype
    )
    return picked.reshape(parts.shape[0], chosen.shape[0], chosen.shape[1] * parts.shape[2])


def collect_parts(received, owner, local, rank, alive, target, capacity, per_device):
    row_count, groups, span_width = received.shape
    block_width = span_width // capacity
    match = ((owner == target) & alive)[:, :, None] & (
        rank[:, :, None] == jnp.arange(capacity)[None, None, :]
    )
    matches = match[:, :, :, None] & (
        local[:, :, None, None] == jnp.arange(per_device)[None, None, None, :]
    )
    onehot = (
        jnp.sum(matches.astype(jnp.int32), axis=1)
        .reshape(groups * capacity, per_device)
        .astype(jnp.bfloat16)
    )
    flattened = received.reshape(row_count, groups * capacity, block_width)
    summed = jnp.einsum("rib,il->rlb", flattened, onehot, preferred_element_type=jnp.float32)
    return summed.reshape(row_count, per_device * block_width)


def on_device(
    dense,
    bottom_weight,
    bottom_bias,
    cross_blocks,
    cross_bias,
    cotangent,
    in_blocks,
    out_blocks,
    live_slots,
):
    groups = lax.axis_size("tensor")
    mine = lax.axis_index("tensor")
    row_count = dense.shape[0]
    local_width = bottom_weight.shape[1]
    per_device = local_width // BLK
    capacity = -(-SLOTS // groups)
    preact = jnp.dot(dense, bottom_weight, preferred_element_type=jnp.float32) + bottom_bias
    start = jax.nn.silu(preact).astype(jnp.bfloat16)
    start_wide = start.astype(jnp.float32)
    cot_wide = cotangent.astype(jnp.float32)
    grad_mixed = cot_wide * start_wide
    grad_mixed_low = grad_mixed.astype(jnp.bfloat16)
    alive = jnp.arange(SLOTS)[None, :] < live_slots[:, None]
    alive_mine = alive[mine]
    switch = alive_mine.astype(jnp.bfloat16)[None, :, None]
    in_owner = in_blocks // per_device
    in_local = in_blocks % per_device
    out_owner = out_blocks // per_device
    out_local = out_blocks % per_device
    in_rank = slot_ranks(in_owner, alive)
    out_rank = slot_ranks(out_owner, alive)
    whole_start = lax.all_gather(start, "tensor", axis=1, tiled=True)
    fetched = jnp.take(whole_start.reshape(row_count, -1, BLK), in_blocks[mine], axis=1)
    taken = fetched
    product = jnp.einsum(
        "rki,kij->rkj",
        taken,
        lax.all_gather(cross_blocks, "dp", axis=1, tiled=True),
        preferred_element_type=jnp.float32,
    )
    parts = product.astype(jnp.bfloat16) * switch
    chosen_out, filled_out = post_table(
        out_owner[mine], out_rank[mine], alive_mine, groups, capacity
    )
    arrived_parts = lax.all_to_all(
        pack_parts(parts, chosen_out, filled_out), "tensor", split_axis=1, concat_axis=1, tiled=True
    )
    mixed = (
        collect_parts(
            arrived_parts, out_owner, out_local, out_rank, alive, mine, capacity, per_device
        )
        + cross_bias
    )
    cross_out = (start_wide * mixed + start_wide).astype(jnp.bfloat16)
    whole_grad = lax.all_gather(grad_mixed_low, "tensor", axis=1, tiled=True)
    upstream = jnp.take(whole_grad.reshape(row_count, -1, BLK), out_blocks[mine], axis=1)
    upstream = upstream * switch
    backward = jnp.einsum(
        "rkj,kij->rki",
        upstream,
        lax.all_gather(cross_blocks, "dp", axis=1, tiled=True),
        preferred_element_type=jnp.float32,
    )
    back_parts = backward.astype(jnp.bfloat16)
    chosen_in, filled_in = post_table(in_owner[mine], in_rank[mine], alive_mine, groups, capacity)
    arrived_back = lax.all_to_all(
        pack_parts(back_parts, chosen_in, filled_in),
        "tensor",
        split_axis=1,
        concat_axis=1,
        tiled=True,
    )
    grad_start = collect_parts(
        arrived_back, in_owner, in_local, in_rank, alive, mine, capacity, per_device
    )
    block_terms = jnp.einsum("rki,rkj->kij", fetched, upstream, preferred_element_type=jnp.float32)
    grad_blocks = lax.psum_scatter(
        block_terms.astype(jnp.bfloat16), "dp", scatter_dimension=1, tiled=True
    ).astype(jnp.float32)
    grad_start = grad_start + cot_wide * mixed + cot_wide
    sigma = jax.nn.sigmoid(preact)
    grad_pre = grad_start * sigma * (1.0 + preact * (1.0 - sigma))
    grad_pre_low = grad_pre.astype(jnp.bfloat16)
    taken = dense
    grad_bottom = lax.psum_scatter(
        lax.dot_general(
            taken, grad_pre_low, (((0,), (0,)), ((), ())), preferred_element_type=jnp.float32
        ).astype(jnp.bfloat16),
        "dp",
        scatter_dimension=0,
        tiled=True,
    ).astype(jnp.float32)
    bias_sums = lax.psum((jnp.sum(grad_pre, axis=0), jnp.sum(grad_mixed, axis=0)), "dp")
    return (cross_out, grad_bottom, bias_sums[0], grad_blocks, bias_sums[1])


def solution(mesh):
    return jax.shard_map(
        on_device,
        mesh=mesh,
        in_specs=(
            P("dp", None),
            P(None, "tensor"),
            P("tensor"),
            P("tensor", "dp", None),
            P("tensor"),
            P("dp", "tensor"),
            P(),
            P(),
            P(),
        ),
        out_specs=(
            P("dp", "tensor"),
            P("dp", "tensor"),
            P("tensor"),
            P("tensor", "dp", None),
            P("tensor"),
        ),
        check_vma=False,
    )
```

profile of v0, /device:TPU:0, one launch (start us, length us, event | category | flops | bytes accessed | tf_op | source)
XLA Modules:
  0.0 400.9 jit_solution(8510571627176802936)
XLA Ops:
  7.2 1.1 copy-done
  8.3 7.8 %fusion.9 = (f32[2048]{0:T(1024)}, bf16[192,2048]{1,0:T(8,128)(2,1)}, f32[192,2048]{1,0:T(8,128)}) fusion(bf16[192,2048]{1,0:T(8,128)(2,1)} %param.18, f32[2048]{0:T(1024)} %param.15, bf16[192,2048]{1,0:T(8,128)(2,1)S(1)} %copy-done, bf16[2048,2048]{1,0:T(8,128)(2,1)} %param.14), kind=kOutput, calls=%fused_computation.28 | convolution fusion | flops 1614542848 | bytes 12337152 | tf_op jit(solution)/shard_map/dot_general | solution.py:72
  16.2 2.3 fusion.10
  18.6 0.7 all-gather.6.cloned.1.call-update
  19.3 0.7 compare_and_fusion.1
  21.2 38.5 %all-gather.4.cloned.1.call-done = bf16[192,16384]{1,0:T(8,128)(2,1)} async-done(((bf16[192,2048]{1,0:T(8,128)(2,1)}), bf16[192,16384]{1,0:T(8,128)(2,1)}) %all-gather.4.cloned.1.call-update) | async-done | bytes 6291472 | tf_op jit(solution)/shard_map/all_gather | solution.py:87
  59.6 6.2 %copy.90 = bf16[24,32,8,512]{3,2,0,1:T(8,128)(2,1)} copy(bf16[24,32,8,512]{3,2,1,0:T(8,128)(2,1)} %bitcast.71) | data formatting | bytes 12582912 | tf_op jit(solution)/shard_map/reshape | solution.py:88
  65.8 37.0 %all-gather.8.cloned.1.call-done = bf16[192,16384]{1,0:T(8,128)(2,1)} async-done(((bf16[192,2048]{1,0:T(8,128)(2,1)}), bf16[192,16384]{1,0:T(8,128)(2,1)}) %all-gather.8.cloned.1.call-update) | async-done | bytes 6291472 | tf_op jit(solution)/shard_map/all_gather | solution.py:110
  102.9 6.3 %copy.89 = bf16[24,32,8,512]{3,2,0,1:T(8,128)(2,1)} copy(bf16[24,32,8,512]{3,2,1,0:T(8,128)(2,1)} %bitcast.72) | data formatting | bytes 12582912 | tf_op jit(solution)/shard_map/reshape | solution.py:111
  109.2 4.9 %gather_fusion = bf16[10,192,512]{2,1,0:T(8,128)(2,1)} fusion(bf16[192,32,512]{2,0,1:T(8,128)(2,1)} %bitcast.69, s32[1024]{0:T(1024)S(1)} %pad_clamp_fusion.3), kind=kCustom, calls=%fused_computation.clone | custom fusion | bytes 3932200 | tf_op jit(solution)/shard_map/jit(_take)/gather | solution.py:88
  114.0 3.7 gather_fusion.2
  117.8 5.8 %convolution_convert_fusion = bf16[10,512,512]{2,1,0:T(8,128)(2,1)} fusion(bf16[10,192,512]{2,1,0:T(8,128)(2,1)} %gather_fusion, pred[10]{0:T(512)(128)(4,1)} %get-tuple-element.65, bf16[10,192,512]{2,1,0:T(8,128)(2,1)S(1)} %gather_fusion.2, pred[10]{0:T(512)(128)(4,1)S(1)} %get-tuple-element.44, bf16[10]{0:T(256)(128)(2,1)} %get-tuple-element.50), kind=kOutput, calls=%fused_computation.9 | convolution fusion | flops 1012203520 | bytes 9175080 | tf_op jit(solution)/shard_map/rki,rkj->kij/dot_general | solution.py:131
  123.6 0.7 copy.56
  124.3 0.7 copy.66
  125.0 1.2 convert_reduce_fusion
  126.4 0.7 fusion.21
  127.7 1.4 fusion.14
  129.7 1.3 copy.61
  131.0 1.4 reshape.262
  132.4 1.5 select_reduce_fusion
  133.8 1.3 copy.59
  135.2 1.3 reshape.253
  136.5 0.7 compare_select_fusion.2
  137.7 1.2 compare_and_fusion.4
  138.9 22.7 %all-gather.6.cloned.1.call-done = bf16[10,512,512]{2,1,0:T(8,128)(2,1)} async-done(((bf16[10,32,512]{2,1,0:T(8,128)(2,1)}), bf16[10,512,512]{2,1,0:T(8,128)(2,1)}) %all-gather.6.cloned.1.call-update) | async-done | bytes 5242896 | tf_op jit(solution)/shard_map/all_gather | solution.py:93
  161.6 5.7 %multiply_bitcast_fusion = bf16[192,10,512]{2,0,1:T(8,128)(2,1)} fusion(bf16[10,512,512]{2,1,0:T(8,128)(2,1)} %all-gather.6.cloned.1.call-done, bf16[10]{0:T(256)(128)(2,1)} %get-tuple-element.50, bf16[10,192,512]{2,1,0:T(8,128)(2,1)} %gather_fusion, pred[10]{0:T(512)(128)(4,1)} %get-tuple-element.65), kind=kOutput, calls=%fused_computation.20 | convolution fusion | flops 1009582080 | bytes 9175070 | tf_op jit(solution)/shard_map/rki,kij->rkj/dot_general | solution.py:90
  167.3 4.0 %gather_fusion.1 = bf16[16,192,512]{2,1,0:T(8,128)(2,1)} fusion(bf16[192,10,512]{2,0,1:T(8,128)(2,1)} %multiply_bitcast_fusion, s32[1024]{0:T(1024)} %pad_clamp_fusion.2), kind=kCustom, calls=%fused_computation.1.clone | custom fusion | bytes 6291520 | tf_op jit(solution)/shard_map/jit(_take)/gather | solution.py:30
  171.4 2.3 bitcast_multiply_fusion.1
  173.6 3.4 copy.62
  177.1 5.7 %reshape.254 = bf16[192,8,1024]{2,1,0:T(8,128)(2,1)} reshape(bf16[192,16,512]{2,1,0:T(8,128)(2,1)} %copy.62) | data formatting | bytes 6291456 | tf_op jit(solution)/shard_map/reshape | solution.py:33
  182.8 5.4 %copy.63 = bf16[192,8,1024]{2,0,1:T(8,128)(2,1)} copy(bf16[192,8,1024]{2,1,0:T(8,128)(2,1)} %reshape.254) | data formatting | bytes 6291456 | tf_op jit(solution)/shard_map/reshape | solution.py:33
  188.1 4.6 %all-to-all-start = ((bf16[192,8,1024]{2,0,1:T(8,128)(2,1)}), bf16[192,8,1024]{2,0,1:T(8,128)(2,1)}, u32[]{:S(2)}, u32[]{:S(2)}) async-start(bf16[192,8,1024]{2,0,1:T(8,128)(2,1)} %copy.63), calls=%async_computation | async-start | bytes 6291456 | tf_op jit(solution)/shard_map/all_to_all | solution.py:100
  192.7 1.2 convert_element_type.138
  193.9 1.3 copy.71
  195.2 1.4 reshape.263
  196.6 1.3 copy.69
  197.9 1.3 reshape.258
  199.2 0.7 compare_select_fusion
  200.5 1.2 compare_and_fusion.2
  201.6 5.8 %convert_bitcast_fusion.1 = bf16[192,10,512]{2,0,1:T(8,128)(2,1)} fusion(bf16[10,512,512]{2,1,0:T(8,128)(2,1)} %all-gather.6.cloned.1.call-done, bf16[10,192,512]{2,1,0:T(8,128)(2,1)S(1)} %gather_fusion.2, pred[10]{0:T(512)(128)(4,1)} %copy-done.21, bf16[10]{0:T(256)(128)(2,1)} %get-tuple-element.50), kind=kOutput, calls=%fused_computation.19 | convolution fusion | flops 1009582080 | bytes 9175070 | tf_op jit(solution)/shard_map/rkj,kij->rki/dot_general | solution.py:113
  207.4 4.1 %gather_fusion.3 = bf16[16,192,512]{2,1,0:T(8,128)(2,1)} fusion(bf16[192,10,512]{2,0,1:T(8,128)(2,1)} %convert_bitcast_fusion.1, s32[1024]{0:T(1024)} %pad_clamp_fusion), kind=kCustom, calls=%fused_computation.3.clone | custom fusion | bytes 6291520 | tf_op jit(solution)/shard_map/jit(_take)/gather | solution.py:30
  211.6 2.3 bitcast_multiply_fusion
  213.8 3.5 copy.72
  217.3 5.7 %reshape.259 = bf16[192,8,1024]{2,1,0:T(8,128)(2,1)} reshape(bf16[192,16,512]{2,1,0:T(8,128)(2,1)} %copy.72) | data formatting | bytes 6291456 | tf_op jit(solution)/shard_map/reshape | solution.py:33
  223.0 5.3 %copy.73 = bf16[192,8,1024]{2,0,1:T(8,128)(2,1)} copy(bf16[192,8,1024]{2,1,0:T(8,128)(2,1)} %reshape.259) | data formatting | bytes 6291456 | tf_op jit(solution)/shard_map/reshape | solution.py:33
  228.3 2.9 all-to-all-done
  231.2 4.4 %all-to-all-start.1 = ((bf16[192,8,1024]{2,0,1:T(8,128)(2,1)}), bf16[192,8,1024]{2,0,1:T(8,128)(2,1)}, u32[]{:S(2)}, u32[]{:S(2)}) async-start(bf16[192,8,1024]{2,0,1:T(8,128)(2,1)} %copy.73), calls=%async_computation.1 | async-start | bytes 6291456 | tf_op jit(solution)/shard_map/all_to_all | solution.py:121
  236.6 5.3 %copy.64 = bf16[192,8,1024]{2,1,0:T(8,128)(2,1)} copy(bf16[192,8,1024]{2,0,1:T(8,128)(2,1)} %all-to-all-done) | data formatting | bytes 6291456 | tf_op jit(solution)/shard_map/all_to_all | solution.py:100
  241.9 5.7 %reshape.255 = bf16[192,16,512]{2,1,0:T(8,128)(2,1)} reshape(bf16[192,8,1024]{2,1,0:T(8,128)(2,1)} %copy.64) | data formatting | bytes 6291456 | tf_op jit(solution)/shard_map/reshape | solution.py:50
  247.6 2.5 fusion.29
  250.7 23.4 %all-to-all-done.1 = bf16[192,8,1024]{2,0,1:T(8,128)(2,1)} async-done(((bf16[192,8,1024]{2,0,1:T(8,128)(2,1)}), bf16[192,8,1024]{2,0,1:T(8,128)(2,1)}, u32[]{:S(2)}, u32[]{:S(2)}) %all-to-all-start.1) | async-done | bytes 3145760 | tf_op jit(solution)/shard_map/all_to_all | solution.py:121
  274.0 5.2 %copy.74 = bf16[192,8,1024]{2,1,0:T(8,128)(2,1)} copy(bf16[192,8,1024]{2,0,1:T(8,128)(2,1)} %all-to-all-done.1) | data formatting | bytes 6291456 | tf_op jit(solution)/shard_map/all_to_all | solution.py:121
  279.3 5.6 %reshape.260 = bf16[192,16,512]{2,1,0:T(8,128)(2,1)} reshape(bf16[192,8,1024]{2,1,0:T(8,128)(2,1)} %copy.74) | data formatting | bytes 6291456 | tf_op jit(solution)/shard_map/reshape | solution.py:50
  284.9 2.5 fusion.30
  287.5 0.6 copy.86
  289.1 1.9 fusion.26
  290.9 5.6 %convert_bitcast_fusion = bf16[2048,2048]{0,1:T(8,128)(2,1)} fusion(bf16[192,2048]{1,0:T(8,128)(2,1)S(1)} %copy-done, bf16[192,2048]{1,0:T(8,128)(2,1)S(1)} %get-tuple-element.43), kind=kOutput, calls=%fused_computation.4 | convolution fusion | flops 1614807040 | bytes 9961472 | tf_op jit(solution)/shard_map/dot_general | solution.py:141
  296.6 12.3 %copy.81 = bf16[2048,2048]{1,0:T(8,128)(2,1)} copy(bf16[2048,2048]{0,1:T(8,128)(2,1)} %convert_bitcast_fusion) | data formatting | bytes 16777216
  308.9 0.7 copy-done.10
  309.5 72.9 %all-reduce = (f32[2048]{0:T(1024)}, f32[2048]{0:T(1024)}) all-reduce(f32[2048]{0:T(1024)S(1)} %get-tuple-element.42, f32[2048]{0:T(1024)S(1)} %copy-done.10), channel_id=1, replica_groups=mesh['dp'=16,'tensor'=8] {'dp'}, use_global_device_ids=true, to_apply=%region_10.13 | all-reduce | flops 4096 | bytes 32768 | tf_op jit(solution)/shard_map/psum | solution.py:148
  382.4 1.9 convert_element_type.136
  384.3 7.5 %reduce-scatter.7.cloned.1.call-done = bf16[128,2048]{1,0:T(8,128)(2,1)} async-done(((bf16[2048,2048]{1,0:T(8,128)(2,1)}), bf16[128,2048]{1,0:T(8,128)(2,1)}) %reduce-scatter.7.cloned.1.call-update) | async-done | bytes 524304
  391.8 1.3 copy.82
  393.1 1.2 copy.76
  (81 shorter events, 6.5 us)
Async XLA Ops:
  7.2 1.1 copy-start
  7.2 9.0 %copy-start.2 = (bf16[192,2048]{1,0:T(8,128)(2,1)S(1)}, bf16[192,2048]{1,0:T(8,128)(2,1)}, u32[]{:S(2)}) copy-start(bf16[192,2048]{1,0:T(8,128)(2,1)} %param.18) | copy-start | bytes 2359300
  7.2 52.4 %all-gather.4.cloned.1.call-start = ((), (), s32[]{:S(2)}) async-start(), calls=%async_computation.4 | async-start | bytes 7077888 | tf_op jit(solution)/shard_map/all_gather | solution.py:87
  16.1 3.2 copy-start.6
  16.1 3.2 copy-start.8
  16.1 3.2 copy-start.20
  16.1 86.8 %all-gather.8.cloned.1.call-start = ((), (), s32[]{:S(2)}) async-start(), calls=%async_computation.6 | async-start | bytes 7077888 | tf_op jit(solution)/shard_map/all_gather | solution.py:110
  18.5 143.1 %all-gather.6.cloned.1.call-start = ((), (), s32[]{:S(2)}) async-start(), calls=%async_computation.5 | async-start | bytes 5570560 | tf_op jit(solution)/shard_map/all_gather | solution.py:93
  19.2 363.2 %reduce-scatter.5.cloned.1.call-start = ((), (), s32[]{:S(2)}) async-start(), calls=%async_computation.7 | async-start | bytes 5570560 | tf_op jit(solution)/shard_map/reduce_scatter | solution.py:132
  20.0 45.9 %copy-start.12 = (pred[8,10]{1,0:T(8,128)(4,1)}, pred[8,10]{1,0:T(8,128)(4,1)S(1)}, u32[]{:S(2)}) copy-start(pred[8,10]{1,0:T(8,128)(4,1)S(1)} %get-tuple-element.57) | copy-start | bytes 244
  20.0 103.6 %copy-start.4 = (s32[8,10]{1,0:T(8,128)}, s32[8,10]{1,0:T(8,128)S(1)}, u32[]{:S(2)}) copy-start(s32[8,10]{1,0:T(8,128)S(1)} %get-tuple-element.53) | copy-start | bytes 964
  20.0 104.3 %copy-start.5 = (s32[8,10]{1,0:T(8,128)}, s32[8,10]{1,0:T(8,128)S(1)}, u32[]{:S(2)}) copy-start(s32[8,10]{1,0:T(8,128)S(1)} %get-tuple-element.56) | copy-start | bytes 964
  21.1 96.6 %copy-start.21 = (pred[10]{0:T(512)(128)(4,1)}, pred[10]{0:T(512)(128)(4,1)S(1)}, u32[]{:S(2)}) copy-start(pred[10]{0:T(512)(128)(4,1)S(1)} %get-tuple-element.44) | copy-start | bytes 34
  127.1 2.0 copy-start.17
  127.1 2.0 copy-start.18
  127.1 0.6 copy-start.15
  127.2 1.9 copy-start.16
  188.1 43.1 %all-to-all-start = ((bf16[192,8,1024]{2,0,1:T(8,128)(2,1)}), bf16[192,8,1024]{2,0,1:T(8,128)(2,1)}, u32[]{:S(2)}, u32[]{:S(2)}) async-start(bf16[192,8,1024]{2,0,1:T(8,128)(2,1)} %copy.63), calls=%async_computation | async-start | bytes 6291456 | tf_op jit(solution)/shard_map/all_to_all | solution.py:100
  207.4 4.2 %copy-start.19 = (bf16[16]{0:T(256)(128)(2,1)S(1)}, bf16[16]{0:T(256)(128)(2,1)}, u32[]{:S(2)}) copy-start(bf16[16]{0:T(256)(128)(2,1)} %reshape.263) | copy-start | bytes 100
  207.4 4.2 %copy-start.22 = (pred[16]{0:T(512)(128)(4,1)S(1)}, pred[16]{0:T(512)(128)(4,1)}, u32[]{:S(2)}) copy-start(pred[16]{0:T(512)(128)(4,1)} %compare_and_fusion.2) | copy-start | bytes 52
  228.3 7.5 %copy-start.7 = (s32[8,10]{1,0:T(8,128)S(1)}, s32[8,10]{1,0:T(8,128)}, u32[]{:S(2)}) copy-start(s32[8,10]{1,0:T(8,128)} %param.20) | copy-start | bytes 964
  228.3 7.5 %copy-start.13 = (pred[8,10]{1,0:T(8,128)(4,1)S(1)}, pred[8,10]{1,0:T(8,128)(4,1)}, u32[]{:S(2)}) copy-start(pred[8,10]{1,0:T(8,128)(4,1)} %get-tuple-element.52) | copy-start | bytes 244
  228.3 7.6 %copy-start.14 = (pred[8,10]{1,0:T(8,128)(4,1)S(1)}, pred[8,10]{1,0:T(8,128)(4,1)}, u32[]{:S(2)}) copy-start(pred[8,10]{1,0:T(8,128)(4,1)} %get-tuple-element.55) | copy-start | bytes 244
  228.3 7.8 %copy-start.9 = (s32[8,10]{1,0:T(8,128)S(1)}, s32[8,10]{1,0:T(8,128)}, u32[]{:S(2)}) copy-start(s32[8,10]{1,0:T(8,128)} %param.19) | copy-start | bytes 964
  231.2 42.9 %all-to-all-start.1 = ((bf16[192,8,1024]{2,0,1:T(8,128)(2,1)}), bf16[192,8,1024]{2,0,1:T(8,128)(2,1)}, u32[]{:S(2)}, u32[]{:S(2)}) async-start(bf16[192,8,1024]{2,0,1:T(8,128)(2,1)} %copy.73), calls=%async_computation.1 | async-start | bytes 6291456 | tf_op jit(solution)/shard_map/all_to_all | solution.py:121
  235.6 156.2 %reduce-scatter.7.cloned.1.call-start = ((), (), s32[]{:S(2)}) async-start(), calls=%async_computation.8 | async-start | bytes 8912896
  287.4 1.1 copy-start.1
  287.4 1.6 copy-start.3
  287.5 1.6 copy-start.11
  308.8 0.7 copy-start.10
Sparse Core Ops, SparseCore 0:
  16.3 43.3 all-gather.3
  61.9 40.9 all-gather.7
  105.0 56.5 all-gather.5
  164.9 78.7 reduce-scatter.4
  309.0 82.7 reduce-scatter.6
where the time goes:
time: 403 us; the launch traced here: 401 us
  waiting for transfers between devices  133 us (33%)
  local copies, waits for them, and re-layouts  113 us (28%)
  blocking collectives  72.9 us (18%)
  matrix products  35.7 us (9%)
  other arithmetic  23.6 us (6%)
  between operations  14.1 us (3%)
  starting transfers between devices  9.25 us (2%)
    psum x1, blocking collectives, on_device(): lax.psum((jnp.sum(grad_pre, axis=0), jnp.sum(grad_mixed, axis=0)), 'dp')  72.9 us
    all_gather x1, waiting for transfers between devices, on_device(): whole_start = lax.all_gather(start, 'tensor', axis=1, tiled=True)  38.5 us
    all_gather x1, waiting for transfers between devices, on_device(): whole_grad = lax.all_gather(grad_mixed_low, 'tensor', axis=1, tiled=True)  37 us
    all_to_all x1, waiting for transfers between devices, on_device(): lax.all_to_all(pack_parts(back_parts, chosen_in, filled_in), 'tensor', sp...  23.4 us
    all_gather x1, waiting for transfers between devices, on_device(): lax.all_gather(cross_blocks, 'dp', axis=1, tiled=True)  22.7 us
    reshape x4, local copies, waits for them, and re-layouts, pack_parts(): picked.reshape(parts.shape[0], chosen.shape[0], chosen.shape[1] * parts.s...  22.1 us
    unnamed x51, local copies, waits for them, and re-layouts  19.4 us
    reshape x2, local copies, waits for them, and re-layouts, collect_parts(): flattened = received.reshape(row_count, groups * capacity, block_width)  11.3 us
  transfers between devices with their start and end apart: 7, of which 6 were waited for; matrix products, arithmetic and copies ran while one was open for 39% of the time, Pallas kernels for 0%

commit v1 on v0

--- a/solution.py
+++ b/solution.py
@@ -97,8 +97,18 @@
     chosen_out, filled_out = post_table(
         out_owner[mine], out_rank[mine], alive_mine, groups, capacity
     )
-    arrived_parts = lax.all_to_all(
-        pack_parts(parts, chosen_out, filled_out), "tensor", split_axis=1, concat_axis=1, tiled=True
+    arrived_parts = jnp.concatenate(
+        lax.all_to_all(
+            jnp.stack(
+                jnp.split(
+                    pack_parts(parts, chosen_out, filled_out), lax.axis_size("tensor"), axis=1
+                )
+            ),
+            "tensor",
+            0,
+            0,
+        ),
+        axis=1,
     )
     mixed = (
         collect_parts(

time: 403 us -> 423 us (1.050)
  waiting for transfers between devices: 133 us -> 150 us
  local copies, waits for them, and re-layouts: 113 us -> 120 us
  other arithmetic: 23.6 us -> 18.5 us
    all_to_all x1, waiting for transfers between devices: 2.85 us -> 23.1 us  [on_device(): lax.all_to_all(jnp.stack(jnp.split(pack_parts(parts, chosen_out, filled_o...]
    split x0 -> x1, local copies, waits for them, and re-layouts: none -> 17.6 us  [on_device(): jnp.split(pack_parts(parts, chosen_out, filled_out), lax.axis_size('tenso...]
    all_gather x1, waiting for transfers between devices: 22.7 us -> 34.2 us  [on_device(): lax.all_gather(cross_blocks, 'dp', axis=1, tiled=True)]
    all_to_all x1, waiting for transfers between devices: 23.4 us -> 13.8 us  [on_device(): lax.all_to_all(pack_parts(back_parts, chosen_in, filled_in), 'tensor', sp...]
    another operation x0 -> x2, local copies, waits for them, and re-layouts: none -> 6.5 us  [the longest x1 5.63 us: collect_parts(): flattened = received.reshape(row_count, groups * capacity, block_width)]
    reshape x2 -> x1, local copies, waits for them, and re-layouts: 11.3 us -> 5.66 us  [collect_parts(): flattened = received.reshape(row_count, groups * capacity, block_width)]
    reshape x4 -> x3, local copies, waits for them, and re-layouts: 22.1 us -> 16.7 us  [pack_parts(): picked.reshape(parts.shape[0], chosen.shape[0], chosen.shape[1] * parts.s...]
    all_to_all x1 -> x0, local copies, waits for them, and re-layouts: 5.28 us -> none  [on_device(): lax.all_to_all(pack_parts(parts, chosen_out, filled_out), 'tensor', split...]
where the time goes in v1:
time: 423 us; the launch traced here: 421 us
  waiting for transfers between devices  150 us (35%)
  local copies, waits for them, and re-layouts  120 us (28%)
  blocking collectives  72.9 us (17%)
  matrix products  35.9 us (8%)
  other arithmetic  18.5 us (4%)
  between operations  14.1 us (3%)
  starting transfers between devices  9.33 us (2%)
    psum x1, blocking collectives, on_device(): lax.psum((jnp.sum(grad_pre, axis=0), jnp.sum(grad_mixed, axis=0)), 'dp')  72.9 us
    all_gather x1, waiting for transfers between devices, on_device(): whole_grad = lax.all_gather(grad_mixed_low, 'tensor', axis=1, tiled=True)  37.1 us
    all_gather x1, waiting for transfers between devices, on_device(): lax.all_gather(cross_blocks, 'dp', axis=1, tiled=True)  34.2 us
    all_gather x1, waiting for transfers between devices, on_device(): whole_start = lax.all_gather(start, 'tensor', axis=1, tiled=True)  33.8 us
    unnamed x44, local copies, waits for them, and re-layouts  23.9 us
    all_to_all x1, waiting for transfers between devices, on_device(): lax.all_to_all(jnp.stack(jnp.split(pack_parts(parts, chosen_out, filled_o...  23.1 us
    split x1, local copies, waits for them, and re-layouts, on_device(): jnp.split(pack_parts(parts, chosen_out, filled_out), lax.axis_size('tenso...  17.6 us
    reshape x3, local copies, waits for them, and re-layouts, pack_parts(): picked.reshape(parts.shape[0], chosen.shape[0], chosen.shape[1] * parts.s...  16.7 us
  transfers between devices with their start and end apart: 7, of which 6 were waited for; matrix products, arithmetic and copies ran while one was open for 39% of the time, Pallas kernels for 0%

profile of v1, /device:TPU:0, one launch (start us, length us, event | category | flops | bytes accessed | tf_op | source)
XLA Modules:
  0.0 421.1 jit_solution(9515800992910145573)
XLA Ops:
  7.2 1.1 copy-done
  8.3 7.8 %fusion.9 = (f32[2048]{0:T(1024)}, bf16[192,2048]{1,0:T(8,128)(2,1)}, f32[192,2048]{1,0:T(8,128)}) fusion(bf16[192,2048]{1,0:T(8,128)(2,1)} %param.18, f32[2048]{0:T(1024)} %param.15, bf16[192,2048]{1,0:T(8,128)(2,1)S(1)} %copy-done, bf16[2048,2048]{1,0:T(8,128)(2,1)} %param.14), kind=kOutput, calls=%fused_computation.28 | convolution fusion | flops 1614542848 | bytes 12337152 | tf_op jit(solution)/shard_map/dot_general | solution.py:72
  16.2 2.3 fusion.10
  18.6 0.7 all-gather.6.cloned.1.call-update
  19.3 0.6 compare_and_fusion.1
  21.6 0.6 reshape.262
  22.3 0.6 reshape.263
  23.3 0.7 reshape.253
  24.0 0.6 compare_and_fusion.3
  24.6 0.6 pad_clamp_fusion.1
  25.2 0.6 pad_clamp_fusion
  25.8 33.8 %all-gather.4.cloned.1.call-done = bf16[192,16384]{1,0:T(8,128)(2,1)} async-done(((bf16[192,2048]{1,0:T(8,128)(2,1)}), bf16[192,16384]{1,0:T(8,128)(2,1)}) %all-gather.4.cloned.1.call-update) | async-done | bytes 6291472 | tf_op jit(solution)/shard_map/all_gather | solution.py:87
  59.6 6.2 %copy.188 = bf16[24,32,8,512]{3,2,0,1:T(8,128)(2,1)} copy(bf16[24,32,8,512]{3,2,1,0:T(8,128)(2,1)} %bitcast.92) | data formatting | bytes 12582912 | tf_op jit(solution)/shard_map/reshape | solution.py:88
  65.8 37.1 %all-gather.8.cloned.1.call-done = bf16[192,16384]{1,0:T(8,128)(2,1)} async-done(((bf16[192,2048]{1,0:T(8,128)(2,1)}), bf16[192,16384]{1,0:T(8,128)(2,1)}) %all-gather.8.cloned.1.call-update) | async-done | bytes 6291472 | tf_op jit(solution)/shard_map/all_gather | solution.py:120
  102.9 6.3 %copy.187 = bf16[24,32,8,512]{3,2,0,1:T(8,128)(2,1)} copy(bf16[24,32,8,512]{3,2,1,0:T(8,128)(2,1)} %bitcast.93) | data formatting | bytes 12582912 | tf_op jit(solution)/shard_map/reshape | solution.py:121
  109.2 4.9 %gather_fusion = bf16[10,192,512]{2,1,0:T(8,128)(2,1)} fusion(bf16[192,32,512]{2,0,1:T(8,128)(2,1)} %bitcast.90, s32[1024]{0:T(1024)S(1)} %pad_clamp_fusion.3), kind=kCustom, calls=%fused_computation.clone | custom fusion | bytes 3932200 | tf_op jit(solution)/shard_map/jit(_take)/gather | solution.py:88
  114.0 3.8 gather_fusion.2
  117.9 5.8 %convolution_convert_fusion = bf16[10,512,512]{2,1,0:T(8,128)(2,1)} fusion(bf16[10,192,512]{2,1,0:T(8,128)(2,1)} %gather_fusion, pred[10]{0:T(512)(128)(4,1)} %get-tuple-element.108, bf16[10,192,512]{2,1,0:T(8,128)(2,1)S(1)} %gather_fusion.2, pred[10]{0:T(512)(128)(4,1)} %get-tuple-element.79, bf16[10]{0:T(256)(128)(2,1)} %get-tuple-element.85), kind=kOutput, calls=%fused_computation.9 | convolution fusion | flops 1012203520 | bytes 9175080 | tf_op jit(solution)/shard_map/rki,rkj->kij/dot_general | solution.py:141
  123.7 0.7 compare_select_fusion.2
  124.4 0.6 pad_clamp_fusion.2
  125.0 1.2 compare_and_fusion.2
  126.2 1.2 compare_and_fusion.4
  127.4 34.2 %all-gather.6.cloned.1.call-done = bf16[10,512,512]{2,1,0:T(8,128)(2,1)} async-done(((bf16[10,32,512]{2,1,0:T(8,128)(2,1)}), bf16[10,512,512]{2,1,0:T(8,128)(2,1)}) %all-gather.6.cloned.1.call-update) | async-done | bytes 5242896 | tf_op jit(solution)/shard_map/all_gather | solution.py:93
  161.6 5.7 %multiply_bitcast_fusion = bf16[192,10,512]{2,0,1:T(8,128)(2,1)} fusion(bf16[10,512,512]{2,1,0:T(8,128)(2,1)} %all-gather.6.cloned.1.call-done, bf16[10]{0:T(256)(128)(2,1)} %get-tuple-element.85, bf16[10,192,512]{2,1,0:T(8,128)(2,1)} %gather_fusion, pred[10]{0:T(512)(128)(4,1)} %get-tuple-element.108), kind=kOutput, calls=%fused_computation.20 | convolution fusion | flops 1009582080 | bytes 9175070 | tf_op jit(solution)/shard_map/rki,kij->rkj/dot_general | solution.py:90
  167.3 4.1 gather_fusion.1
  171.4 2.3 bitcast_multiply_fusion.1
  173.6 3.4 copy.145
  177.0 5.7 %reshape.254 = bf16[192,8,1024]{2,1,0:T(8,128)(2,1)} reshape(bf16[192,16,512]{2,1,0:T(8,128)(2,1)} %copy.145) | data formatting | bytes 6291456 | tf_op jit(solution)/shard_map/reshape | solution.py:33
  182.7 5.8 %convert_bitcast_fusion.1 = bf16[192,10,512]{2,0,1:T(8,128)(2,1)} fusion(bf16[10,512,512]{2,1,0:T(8,128)(2,1)} %all-gather.6.cloned.1.call-done, bf16[10,192,512]{2,1,0:T(8,128)(2,1)S(1)} %gather_fusion.2, pred[10]{0:T(512)(128)(4,1)} %get-tuple-element.79, bf16[10]{0:T(256)(128)(2,1)} %get-tuple-element.85), kind=kOutput, calls=%fused_computation.19 | convolution fusion | flops 1009582080 | bytes 9175070 | tf_op jit(solution)/shard_map/rkj,kij->rki/dot_general | solution.py:123
  188.5 4.1 gather_fusion.3
  192.6 2.3 bitcast_multiply_fusion
  194.9 3.4 copy.154
  198.3 5.7 %reshape.259 = bf16[192,8,1024]{2,1,0:T(8,128)(2,1)} reshape(bf16[192,16,512]{2,1,0:T(8,128)(2,1)} %copy.154) | data formatting | bytes 6291456 | tf_op jit(solution)/shard_map/reshape | solution.py:33
  204.0 5.3 %copy.155 = bf16[192,8,1024]{2,0,1:T(8,128)(2,1)} copy(bf16[192,8,1024]{2,1,0:T(8,128)(2,1)} %reshape.259) | data formatting | bytes 6291456 | tf_op jit(solution)/shard_map/reshape | solution.py:33
  209.3 4.5 %all-to-all-start.1 = ((bf16[192,8,1024]{2,0,1:T(8,128)(2,1)}), bf16[192,8,1024]{2,0,1:T(8,128)(2,1)}, u32[]{:S(2)}, u32[]{:S(2)}) async-start(bf16[192,8,1024]{2,0,1:T(8,128)(2,1)} %copy.155), calls=%async_computation.1 | async-start | bytes 6291456 | tf_op jit(solution)/shard_map/all_to_all | solution.py:131
  213.7 17.6 %fusion.29 = (bf16[192,1,1024]{2,1,0:T(2,128)(2,1)S(1)}, bf16[192,1,1024]{2,1,0:T(2,128)(2,1)S(1)}, bf16[192,1,1024]{2,1,0:T(2,128)(2,1)S(1)}, bf16[192,1,1024]{...) fusion(bf16[192,8,1024]{2,1,0:T(8,128)(2,1)} %reshape.254), kind=kLoop, calls=%fused_computation.106 | loop fusion | bytes 6291456 | tf_op jit(solution)/shard_map/split | solution.py:103
  231.4 0.9 bitcast_dynamic-update-slice_fusion.7
  232.2 0.9 bitcast_dynamic-update-slice_fusion.6
  233.1 0.9 bitcast_dynamic-update-slice_fusion.5
  234.0 0.9 bitcast_dynamic-update-slice_fusion.4
  234.9 0.9 bitcast_dynamic-update-slice_fusion.3
  235.8 0.9 bitcast_dynamic-update-slice_fusion.2
  236.6 0.9 bitcast_dynamic-update-slice_fusion.1
  237.5 0.9 bitcast_dynamic-update-slice_fusion
  238.4 13.8 %all-to-all-done.1 = bf16[192,8,1024]{2,0,1:T(8,128)(2,1)} async-done(((bf16[192,8,1024]{2,0,1:T(8,128)(2,1)}), bf16[192,8,1024]{2,0,1:T(8,128)(2,1)}, u32[]{:S(2)}, u32[]{:S(2)}) %all-to-all-start.1) | async-done | bytes 3145760 | tf_op jit(solution)/shard_map/all_to_all | solution.py:131
  252.2 4.5 %all-to-all-start = ((bf16[8,192,1,1024]{3,1,2,0:T(8,128)(2,1)}), bf16[8,192,1,1024]{3,1,2,0:T(8,128)(2,1)}, u32[]{:S(2)}, u32[]{:S(2)}) async-start(bf16[8,192,1,1024]{3,1,2,0:T(8,128)(2,1)} %bitcast_dynamic-update-slice_fusion), calls=%async_computation | async-start | bytes 6291456 | tf_op jit(solution)/shard_map/all_to_all | solution.py:101
  257.8 5.3 %copy.156 = bf16[192,8,1024]{2,1,0:T(8,128)(2,1)} copy(bf16[192,8,1024]{2,0,1:T(8,128)(2,1)} %all-to-all-done.1) | data formatting | bytes 6291456 | tf_op jit(solution)/shard_map/all_to_all | solution.py:131
  263.2 5.7 %reshape.260 = bf16[192,16,512]{2,1,0:T(8,128)(2,1)} reshape(bf16[192,8,1024]{2,1,0:T(8,128)(2,1)} %copy.156) | data formatting | bytes 6291456 | tf_op jit(solution)/shard_map/reshape | solution.py:50
  268.8 2.5 fusion.31
  271.3 0.6 copy.176
  271.9 23.1 %all-to-all-done = bf16[8,192,1,1024]{3,1,2,0:T(8,128)(2,1)} async-done(((bf16[8,192,1,1024]{3,1,2,0:T(8,128)(2,1)}), bf16[8,192,1,1024]{3,1,2,0:T(8,128)(2,1)}, u32[]{:S(2)}, u32[]{:S(2)}) %all-to-all-start) | async-done | bytes 3145760 | tf_op jit(solution)/shard_map/all_to_all | solution.py:101
  295.1 5.3 %copy.146 = bf16[192,8,1,1024]{3,1,0,2:T(8,128)(2,1)} copy(bf16[192,8,1,1024]{3,0,2,1:T(8,128)(2,1)} %bitcast.8) | data formatting | bytes 6291456 | tf_op jit(solution)/shard_map/reshape | solution.py:100
  300.3 5.6 %reshape_reshape.3 = bf16[192,16,512]{2,1,0:T(8,128)(2,1)} reshape(bf16[192,8,1,1024]{3,1,0,2:T(8,128)(2,1)} %copy.146) | data formatting | bytes 6291456 | tf_op jit(solution)/shard_map/reshape;reshape | solution.py:50
  306.0 2.7 fusion.30
  308.6 0.6 copy.175
  309.3 1.9 fusion.26
  311.1 5.6 %convert_bitcast_fusion = bf16[2048,2048]{0,1:T(8,128)(2,1)} fusion(bf16[192,2048]{1,0:T(8,128)(2,1)S(1)} %copy-done, bf16[192,2048]{1,0:T(8,128)(2,1)S(1)} %get-tuple-element.78), kind=kOutput, calls=%fused_computation.4 | convolution fusion | flops 1614807040 | bytes 9961472 | tf_op jit(solution)/shard_map/dot_general | solution.py:151
  316.8 12.3 %copy.163 = bf16[2048,2048]{1,0:T(8,128)(2,1)} copy(bf16[2048,2048]{0,1:T(8,128)(2,1)} %convert_bitcast_fusion) | data formatting | bytes 16777216
  329.0 0.7 copy-done.8
  329.7 72.9 %all-reduce = (f32[2048]{0:T(1024)}, f32[2048]{0:T(1024)}) all-reduce(f32[2048]{0:T(1024)S(1)} %get-tuple-element.77, f32[2048]{0:T(1024)S(1)} %copy-done.8), channel_id=1, replica_groups=mesh['dp'=16,'tensor'=8] {'dp'}, use_global_device_ids=true, to_apply=%region_10.13 | all-reduce | flops 4096 | bytes 32768 | tf_op jit(solution)/shard_map/psum | solution.py:158
  402.6 1.9 convert_element_type.136
  404.5 7.5 %reduce-scatter.7.cloned.1.call-done = bf16[128,2048]{1,0:T(8,128)(2,1)} async-done(((bf16[2048,2048]{1,0:T(8,128)(2,1)}), bf16[128,2048]{1,0:T(8,128)(2,1)}) %reduce-scatter.7.cloned.1.call-update) | async-done | bytes 524304
  412.0 1.3 copy.164
  413.4 1.2 copy.158
  (75 shorter events, 3.6 us)
Async XLA Ops:
  7.2 1.1 copy-start
  7.2 9.0 %copy-start.2 = (bf16[192,2048]{1,0:T(8,128)(2,1)S(1)}, bf16[192,2048]{1,0:T(8,128)(2,1)}, u32[]{:S(2)}) copy-start(bf16[192,2048]{1,0:T(8,128)(2,1)} %param.18) | copy-start | bytes 2359300
  7.2 52.4 %all-gather.4.cloned.1.call-start = ((), (), s32[]{:S(2)}) async-start(), calls=%async_computation.4 | async-start | bytes 7077888 | tf_op jit(solution)/shard_map/all_gather | solution.py:87
  16.1 3.2 copy-start.4
  16.1 3.2 copy-start.6
  16.1 3.2 copy-start.13
  16.1 86.8 %all-gather.8.cloned.1.call-start = ((), (), s32[]{:S(2)}) async-start(), calls=%async_computation.6 | async-start | bytes 7077888 | tf_op jit(solution)/shard_map/all_gather | solution.py:120
  18.5 143.1 %all-gather.6.cloned.1.call-start = ((), (), s32[]{:S(2)}) async-start(), calls=%async_computation.5 | async-start | bytes 5570560 | tf_op jit(solution)/shard_map/all_gather | solution.py:93
  19.2 383.4 %reduce-scatter.5.cloned.1.call-start = ((), (), s32[]{:S(2)}) async-start(), calls=%async_computation.7 | async-start | bytes 5570560 | tf_op jit(solution)/shard_map/reduce_scatter | solution.py:142
  23.2 42.6 %copy-start.14 = (s32[16]{0:T(128)}, s32[16]{0:T(128)S(1)}, u32[]{:S(2)}) copy-start(s32[16]{0:T(128)S(1)} %reshape.258) | copy-start | bytes 196
  188.5 4.1 copy-start.12
  188.5 4.1 copy-start.15
  209.3 42.9 %all-to-all-start.1 = ((bf16[192,8,1024]{2,0,1:T(8,128)(2,1)}), bf16[192,8,1024]{2,0,1:T(8,128)(2,1)}, u32[]{:S(2)}, u32[]{:S(2)}) async-start(bf16[192,8,1024]{2,0,1:T(8,128)(2,1)} %copy.155), calls=%async_computation.1 | async-start | bytes 6291456 | tf_op jit(solution)/shard_map/all_to_all | solution.py:131
  238.4 18.7 %copy-start.5 = (s32[8,10]{1,0:T(8,128)S(1)}, s32[8,10]{1,0:T(8,128)}, u32[]{:S(2)}) copy-start(s32[8,10]{1,0:T(8,128)} %param.20) | copy-start | bytes 964
  238.4 18.7 %copy-start.10 = (pred[8,10]{1,0:T(8,128)(4,1)S(1)}, pred[8,10]{1,0:T(8,128)(4,1)}, u32[]{:S(2)}) copy-start(pred[8,10]{1,0:T(8,128)(4,1)} %get-tuple-element.87) | copy-start | bytes 244
  238.4 18.7 %copy-start.11 = (pred[8,10]{1,0:T(8,128)(4,1)S(1)}, pred[8,10]{1,0:T(8,128)(4,1)}, u32[]{:S(2)}) copy-start(pred[8,10]{1,0:T(8,128)(4,1)} %get-tuple-element.98) | copy-start | bytes 244
  238.4 19.0 %copy-start.7 = (s32[8,10]{1,0:T(8,128)S(1)}, s32[8,10]{1,0:T(8,128)}, u32[]{:S(2)}) copy-start(s32[8,10]{1,0:T(8,128)} %param.19) | copy-start | bytes 964
  252.2 42.9 %all-to-all-start = ((bf16[8,192,1,1024]{3,1,2,0:T(8,128)(2,1)}), bf16[8,192,1,1024]{3,1,2,0:T(8,128)(2,1)}, u32[]{:S(2)}, u32[]{:S(2)}) async-start(bf16[8,192,1,1024]{3,1,2,0:T(8,128)(2,1)} %bitcast_dynamic-update-slice_fusion), calls=%async_computation | async-start | bytes 6291456 | tf_op jit(solution)/shard_map/all_to_all | solution.py:101
  256.6 155.4 %reduce-scatter.7.cloned.1.call-start = ((), (), s32[]{:S(2)}) async-start(), calls=%async_computation.8 | async-start | bytes 8912896
  306.0 3.3 copy-start.1
  306.0 3.3 copy-start.3
  306.0 3.3 copy-start.9
  329.0 0.7 copy-start.8
Sparse Core Ops, SparseCore 0:
  16.3 43.3 all-gather.3
  61.9 40.9 all-gather.7
  105.0 56.5 all-gather.5
  164.9 78.7 reduce-scatter.4
  329.2 82.8 reduce-scatter.6
